TPU v7x, 32 devices: a whole 2x2x4 slice. The times are simulated.
32 devices in a mesh: area: 4 (over y, core), pos: 8 (over z, x).
Axes of the slice: x: 2, y: 2, z: 4, core: 2. Of those that a mesh axis runs over, the one named last changes fastest.
Arguments:
- exit_wave: bfloat16 [128, 2, 128, 128], P(('area', 'pos')), may hold values from -6 to 6
- amplitude: bfloat16 [128, 128, 128], P(('area', 'pos')), may hold values from 0.19921875 to 5
- probe: float32 [2, 128, 128], replicated, may hold values from -4 to 4
- offsets: int32 [128, 2], P(('area', 'pos')), may hold values from 0 to 127
- owner: int32 [128, 1], P(('area', 'pos')), may hold values from 0 to 7; in each aligned block of 4 rows (0 to 3, 4 to 7, ...) at most 2 rows name the same one
Outputs:
- new_wave: bfloat16 [128, 2, 128, 128], P(('area', 'pos'))
- object_field: float32 [2, 512, 1024], P(None, 'area', 'pos')
Inputs may be any that keep to these rules, and one draw needn't show every extreme that they name: owner names the object tile column that holds the position's patch centre; of the 4 positions of one device at most 2 name the same tile.
All inputs are finite; a program needn't handle non-finite values.
Results may differ from a plain program's by a relative error of at most 0.0059.
Values may be sent and summed in bfloat16 or wider, within the bound.
No kernel may reach another device: no remote copies, remote signals or barrier semaphores. Data moves between devices by JAX's collectives and lax.ppermute only.
A program may use at most 64 MiB of HBM per device.

v0:
```python
import math
import jax
import jax.numpy as jnp
from jax import lax
from jax.sharding import PartitionSpec as P

F = 128
TS = 128
C = 2


def passed_along(value, axis, steps):
    count = lax.axis_size(axis)
    first, last = (max(0, -steps), min(count, count - steps))
    return lax.ppermute(value, axis, [(source, source + steps) for source in range(first, last)])


def extended(cells, sides, width):
    for axis, dim in sides:
        count = lax.axis_size(axis)
        ends = count - 1
        head = lax.slice_in_dim(cells, 0, width, axis=dim)
        tail = lax.slice_in_dim(cells, cells.shape[dim] - width, cells.shape[dim], axis=dim)
        cells = jnp.concatenate(
            [
                lax.ppermute(tail, axis, [(i, (i + 1) % count) for i in range(ends)]),
                cells,
                lax.ppermute(head, axis, [((i + 1) % count, i) for i in range(ends)]),
            ],
            axis=dim,
        )
    return cells


def fold_rows(canvas):
    margin = F // 2
    summed = canvas
    for step in (1, -1):
        edge = canvas[:, TS + margin :, :] if step == 1 else canvas[:, :margin, :]
        arrived = passed_along(edge, "area", step)
        first = margin if step == 1 else TS
        summed = summed.at[:, first : first + margin, :].add(arrived)
    return summed[:, margin : margin + TS, :]


def fold_columns(canvas):
    margin = F // 2
    summed = canvas
    for step in (1, -1):
        edge = canvas[:, :, TS + margin :] if step == 1 else canvas[:, :, :margin]
        arrived = passed_along(edge, "pos", step)
        first = margin if step == 1 else TS
        summed = summed.at[:, :, first : first + margin].add(arrived)
    return summed[:, :, margin : margin + TS]


def left_multiply(mat_re, mat_im, data_re, data_im):
    highest = lax.Precision.HIGHEST
    out_re = jnp.einsum("kn,bnm->bkm", mat_re, data_re, precision=highest) - jnp.einsum(
        "kn,bnm->bkm", mat_im, data_im, precision=highest
    )
    out_im = jnp.einsum("kn,bnm->bkm", mat_re, data_im, precision=highest) + jnp.einsum(
        "kn,bnm->bkm", mat_im, data_re, precision=highest
    )
    return (out_re, out_im)


def right_multiply(data_re, data_im, mat_re, mat_im):
    highest = lax.Precision.HIGHEST
    out_re = jnp.einsum("bkm,ml->bkl", data_re, mat_re, precision=highest) - jnp.einsum(
        "bkm,ml->bkl", data_im, mat_im, precision=highest
    )
    out_im = jnp.einsum("bkm,ml->bkl", data_re, mat_im, precision=highest) + jnp.einsum(
        "bkm,ml->bkl", data_im, mat_re, precision=highest
    )
    return (out_re, out_im)


def cut_patches(source, row_starts, col_starts):
    return jax.vmap(lambda r, c: lax.dynamic_slice(source, (jnp.int32(0), r, c), (2, F, F)))(
        row_starts, col_starts
    )


def weighted_waves(waves_bf, probe_re, probe_im):
    waves_f = waves_bf.astype(jnp.float32)
    first = probe_re * waves_f[:, 0] + probe_im * waves_f[:, 1]
    second = probe_re * waves_f[:, 1] - probe_im * waves_f[:, 0]
    return jnp.stack([first, second], 1).astype(jnp.bfloat16)


def accumulate(contrib, meta, power_map):
    live = meta[:, 2]
    ordering = jnp.argsort(1 - live, stable=True)
    live_count = jnp.sum(live)

    def add_one(number, canvas):
        chosen = ordering[number]
        piece = jnp.concatenate([contrib[chosen].astype(jnp.float32), power_map[None]], 0)
        where = (jnp.int32(0), meta[chosen, 0], meta[chosen, 1])
        old = lax.dynamic_slice(canvas, where, (3, F, F))
        return lax.dynamic_update_slice(canvas, old + piece, where)

    canvas = lax.fori_loop(0, live_count, add_one, jnp.zeros((3, TS + F, TS + F), jnp.float32))
    summed = fold_columns(fold_rows(canvas))
    return (summed[0:2] / (summed[2] + 0.1)[None], ordering, live_count)


def relaxed_update(waves_bf, amps_bf, patch_bf, probe_re, probe_im):
    pixel = jnp.arange(F, dtype=jnp.int32)
    product = pixel[:, None] * pixel[None, :] % F
    angle = product.astype(jnp.float32) * (2.0 * math.pi / F)
    scale_by = 1.0 / math.sqrt(F)
    twiddle_re = jnp.cos(angle) * scale_by
    twiddle_im = -jnp.sin(angle) * scale_by
    waves_f = waves_bf.astype(jnp.float32)
    patch_f = patch_bf.astype(jnp.float32)
    proj_re = probe_re * patch_f[:, 0] - probe_im * patch_f[:, 1]
    proj_im = probe_re * patch_f[:, 1] + probe_im * patch_f[:, 0]
    trial_re = 2.0 * proj_re - waves_f[:, 0]
    trial_im = 2.0 * proj_im - waves_f[:, 1]
    half_re, half_im = left_multiply(twiddle_re, twiddle_im, trial_re, trial_im)
    spectrum_re, spectrum_im = right_multiply(half_re, half_im, twiddle_re, twiddle_im)
    modulus = jnp.sqrt(spectrum_re * spectrum_re + spectrum_im * spectrum_im + 0.01)
    ratio = amps_bf.astype(jnp.float32) / modulus
    fitted_re = spectrum_re * ratio
    fitted_im = spectrum_im * ratio
    half_re, half_im = left_multiply(twiddle_re, -twiddle_im, fitted_re, fitted_im)
    back_re, back_im = right_multiply(half_re, half_im, twiddle_re, -twiddle_im)
    new_re = 0.75 * waves_f[:, 0] - 0.5 * proj_re + 0.75 * back_re
    new_im = 0.75 * waves_f[:, 1] - 0.5 * proj_im + 0.75 * back_im
    return jnp.stack([new_re, new_im], 1).astype(jnp.bfloat16)


def body(exit_wave, amplitude, probe, offsets, owner):
    margin = F // 2
    columns_count = lax.axis_size("pos")
    probe_re = probe[0]
    probe_im = probe[1]
    power_map = probe_re * probe_re + probe_im * probe_im
    target = owner[:, 0]
    one_hot = (target[:, None] == jnp.arange(columns_count, dtype=jnp.int32)[None, :]).astype(
        jnp.int32
    )
    rank_in = jnp.sum((jnp.cumsum(one_hot, axis=0) - 1) * one_hot, axis=1)
    slot_flat = target * C + rank_in
    slot_total = columns_count * C
    described = jnp.concatenate([offsets, jnp.ones((offsets.shape[0], 1), jnp.int32)], 1)
    send_meta = jnp.zeros((slot_total, 3), jnp.int32).at[slot_flat].set(described)
    contrib = weighted_waves(exit_wave, probe_re, probe_im)
    send_wave = jnp.zeros((slot_total, 2, F, F), jnp.bfloat16).at[slot_flat].set(contrib)
    got_wave, got_meta = (
        lax.all_to_all(send_wave, "pos", split_axis=0, concat_axis=0, tiled=True),
        lax.all_to_all(send_meta, "pos", split_axis=0, concat_axis=0, tiled=True),
    )
    object_tile, ordering, live_count = accumulate(got_wave, got_meta, power_map)
    object_half = object_tile.astype(jnp.bfloat16)
    strip = extended(object_half, (("area", 1),), margin)
    band_rows = lax.all_gather(strip, "pos", axis=2, tiled=True)
    band_rows = jnp.pad(band_rows, ((0, 0), (0, 0), (margin, margin)))
    own_patch = cut_patches(band_rows, offsets[:, 0], target * TS + offsets[:, 1])
    new_wave = relaxed_update(exit_wave, amplitude, own_patch, probe_re, probe_im)
    return (new_wave, object_tile)


def solution(mesh):
    return jax.shard_map(
        body,
        mesh=mesh,
        in_specs=(
            P(("area", "pos"), None, None, None),
            P(("area", "pos"), None, None),
            P(),
            P(("area", "pos"), None),
            P(("area", "pos"), None),
        ),
        out_specs=(P(("area", "pos"), None, None, None), P(None, "area", "pos")),
        check_vma=False,
    )
```

profile of v0, /device:TPU:0, one launch (start us, length us, event | category | flops | bytes accessed | tf_op | source)
XLA Modules:
  0.0 265.7 jit_solution(17552448648142886674)
XLA Ops:
  7.9 0.8 select_reduce_fusion
  8.8 0.8 copy.121
  9.5 0.8 compare_select_fusion.1
  10.3 1.2 scatter_custom_fusion
  11.5 7.3 %all-to-all-start = ((s32[8,2,3]{2,1,0:T(2,128)}), s32[8,2,3]{2,1,0:T(2,128)S(1)}, u32[]{:S(2)}, u32[]{:S(2)}) async-start(s32[8,2,3]{2,1,0:T(2,128)} %bitcast.10), calls=%async_computation | async-start | bytes 16384 | tf_op jit(solution)/shard_map/all_to_all | solution.py:154
  18.7 1.0 copy_convert_fusion
  19.7 0.9 slice_bitcast_fusion.3
  20.8 1.2 broadcast_in_dim.11
  22.0 2.2 scatter_fusion
  24.2 1.1 all-to-all-done
  25.3 5.0 %all-to-all-start.1 = ((bf16[16,2,128,128]{3,2,1,0:T(8,128)(2,1)}), bf16[16,2,128,128]{3,2,1,0:T(8,128)(2,1)S(1)}, u32[]{:S(2)}, u32[]{:S(2)}) async-start(bf16[16,2,128,128]{3,2,1,0:T(8,128)(2,1)} %scatter_fusion), calls=%async_computation.1 | async-start | bytes 2097152 | tf_op jit(solution)/shard_map/all_to_all | solution.py:153
  31.1 1.3 sort.17
  32.3 23.4 %all-to-all-done.1 = bf16[16,2,128,128]{3,2,1,0:T(8,128)(2,1)S(1)} async-done(((bf16[16,2,128,128]{3,2,1,0:T(8,128)(2,1)}), bf16[16,2,128,128]{3,2,1,0:T(8,128)(2,1)S(1)}, u32[]{:S(2)}, u32[]{:S(2)}) %all-to-all-start.1) | async-done | bytes 1048608 | tf_op jit(solution)/shard_map/all_to_all | solution.py:153
  55.8 62.8 %while.15 = (s32[]{:T(128)}, f32[3,256,256]{2,1,0:T(8,128)S(1)}, s32[]{:T(128)}, s32[16]{0:T(128)S(1)}, s32[16,3]{0,1:T(4,128)S(1)}, /*index=5*/bf16[16,2,128,12...) while((s32[]{:T(128)}, f32[3,256,256]{2,1,0:T(8,128)S(1)}, ...), condition=%wide.region_7.8_spmd, body=%wide.region_6.7_spmd.sunk | while | flops 131086 | bytes 1179941 | solution.py:104
  63.3 2.8 %dynamic_update_slice.4 = f32[3,256,256]{2,1,0:T(8,128)S(1)} dynamic-update-slice(f32[3,256,256]{2,1,0:T(8,128)S(1)} %get-tuple-element.257, f32[3,128,128]{2,1,0:T(8,128)S(1)} %maximum_add_fusion.2, s32[]{:T(128)} %constant.154.clone.1..sunk, s32[]{:T(128)S(6)} %select_n.138, s32[]{:T(128)S(6)} %select_n.139) | dynamic-update-slice | bytes 393220 | tf_op jit(solution)/shard_map/while/body/dynamic_update_slice | solution.py:102
  73.5 2.9 %dynamic_update_slice.4 = f32[3,256,256]{2,1,0:T(8,128)S(1)} dynamic-update-slice(f32[3,256,256]{2,1,0:T(8,128)S(1)} %get-tuple-element.257, f32[3,128,128]{2,1,0:T(8,128)S(1)} %maximum_add_fusion.2, s32[]{:T(128)} %constant.154.clone.1..sunk, s32[]{:T(128)S(6)} %select_n.138, s32[]{:T(128)S(6)} %select_n.139) | dynamic-update-slice | bytes 393220 | tf_op jit(solution)/shard_map/while/body/dynamic_update_slice | solution.py:102
  83.9 2.9 %dynamic_update_slice.4 = f32[3,256,256]{2,1,0:T(8,128)S(1)} dynamic-update-slice(f32[3,256,256]{2,1,0:T(8,128)S(1)} %get-tuple-element.257, f32[3,128,128]{2,1,0:T(8,128)S(1)} %maximum_add_fusion.2, s32[]{:T(128)} %constant.154.clone.1..sunk, s32[]{:T(128)S(6)} %select_n.138, s32[]{:T(128)S(6)} %select_n.139) | dynamic-update-slice | bytes 393220 | tf_op jit(solution)/shard_map/while/body/dynamic_update_slice | solution.py:102
  94.3 2.8 %dynamic_update_slice.4 = f32[3,256,256]{2,1,0:T(8,128)S(1)} dynamic-update-slice(f32[3,256,256]{2,1,0:T(8,128)S(1)} %get-tuple-element.257, f32[3,128,128]{2,1,0:T(8,128)S(1)} %maximum_add_fusion.2, s32[]{:T(128)} %constant.154.clone.1..sunk, s32[]{:T(128)S(6)} %select_n.138, s32[]{:T(128)S(6)} %select_n.139) | dynamic-update-slice | bytes 393220 | tf_op jit(solution)/shard_map/while/body/dynamic_update_slice | solution.py:102
  104.5 3.0 %dynamic_update_slice.4 = f32[3,256,256]{2,1,0:T(8,128)S(1)} dynamic-update-slice(f32[3,256,256]{2,1,0:T(8,128)S(1)} %get-tuple-element.257, f32[3,128,128]{2,1,0:T(8,128)S(1)} %maximum_add_fusion.2, s32[]{:T(128)} %constant.154.clone.1..sunk, s32[]{:T(128)S(6)} %select_n.138, s32[]{:T(128)S(6)} %select_n.139) | dynamic-update-slice | bytes 393220 | tf_op jit(solution)/shard_map/while/body/dynamic_update_slice | solution.py:102
  115.0 2.9 %dynamic_update_slice.4 = f32[3,256,256]{2,1,0:T(8,128)S(1)} dynamic-update-slice(f32[3,256,256]{2,1,0:T(8,128)S(1)} %get-tuple-element.257, f32[3,128,128]{2,1,0:T(8,128)S(1)} %maximum_add_fusion.2, s32[]{:T(128)} %constant.154.clone.1..sunk, s32[]{:T(128)S(6)} %select_n.138, s32[]{:T(128)S(6)} %select_n.139) | dynamic-update-slice | bytes 393220 | tf_op jit(solution)/shard_map/while/body/dynamic_update_slice | solution.py:102
  118.6 1.3 collective-permute-start
  119.9 1.0 collective-permute-done
  121.0 1.3 collective-permute-start.1
  122.3 2.0 collective-permute-done.1
  124.5 1.3 collective-permute-start.2
  125.9 1.3 collective-permute-start.3
  127.2 1.8 collective-permute-done.2
  129.1 1.3 scatter-add.16
  130.5 54.6 %collective-permute-done.3 = f32[3,128,64]{2,1,0:T(8,128)S(1)} collective-permute-done((f32[3,128,64]{2,1,0:T(8,128)S(1)}, f32[3,128,64]{2,1,0:T(8,128)S(1)}, u32[]{:S(2)}, u32[]{:S(2)}) %collective-permute-start.3) | collective-permute-done | bytes 98336 | tf_op jit(solution)/shard_map/ppermute | solution.py:15
  185.6 0.8 fusion.145
  186.4 4.8 %collective-permute-start.4 = (bf16[2,64,128]{2,1,0:T(8,128)(2,1)S(1)}, bf16[2,64,128]{2,1,0:T(8,128)(2,1)S(1)}, u32[]{:S(2)}, u32[]{:S(2)}) collective-permute-start(bf16[2,64,128]{2,1,0:T(8,128)(2,1)S(1)} %get-tuple-element.161), channel_id=1, source_target_pairs={{0,8},{8,16},{16,24},{1,9},{9,17},{17,25},{2,10},{10,18},{18,26},{... | collective-permute-start | bytes 98312 | tf_op jit(solution)/shard_map/ppermute | solution.py:26
  191.2 1.3 collective-permute-start.5
  192.5 2.3 collective-permute-done.5
  195.6 40.4 %all-gather.2.cloned.1.call-done = bf16[2,256,1024]{2,1,0:T(8,128)(2,1)} async-done(((bf16[2,256,128]{2,1,0:T(8,128)(2,1)}), bf16[2,256,1024]{2,1,0:T(8,128)(2,1)}) %all-gather.2.cloned.1.call-update) | async-done | bytes 1048592 | tf_op jit(solution)/shard_map/all_gather | solution.py:159
  236.0 1.9 pad.13
  237.9 8.0 %while.16 = (s32[]{:T(128)}, bf16[2,256,1152]{2,1,0:T(8,128)(2,1)S(1)}, s32[4,3]{1,0:T(4,128)S(1)}, bf16[4,2,128,128]{3,2,0,1:T(8,128)(2,1)S(1)}, s32[]{:T(128)}) while((s32[]{:T(128)}, bf16[2,256,1152]{2,1,0:T(8,128)(2,1)S(1)}, s32[4,3]{1,0:T(4,128)S(1)}, bf16[4,2,128,128]{3,2,0,1:T(8,128)(2,1)S(1)}, s32[]{:T(128)}) %tuple.76), condition=%wide.while_cond.4, body=%wide.while_body.4.sunk | while | flops 2 | bytes 131189 | solution.py:80
  238.5 1.3 bitcast_dynamic-update-slice_fusion.2
  240.5 1.3 bitcast_dynamic-update-slice_fusion.2
  242.4 1.3 bitcast_dynamic-update-slice_fusion.2
  244.3 1.3 bitcast_dynamic-update-slice_fusion.2
  246.0 0.7 fusion.18
  246.8 0.8 fusion.17
  247.5 0.8 fusion.7
  249.7 0.7 fusion.6
  252.0 0.8 fusion.34
  252.8 0.8 fusion.38
  253.6 0.8 fusion.5
  255.8 0.8 fusion.4
  (76 shorter events, 20.9 us)
Async XLA Ops:
  11.5 13.8 %all-to-all-start = ((s32[8,2,3]{2,1,0:T(2,128)}), s32[8,2,3]{2,1,0:T(2,128)S(1)}, u32[]{:S(2)}, u32[]{:S(2)}) async-start(s32[8,2,3]{2,1,0:T(2,128)} %bitcast.10), calls=%async_computation | async-start | bytes 16384 | tf_op jit(solution)/shard_map/all_to_all | solution.py:154
  24.2 6.2 %copy-start.1 = (f32[2,128,128]{2,1,0:T(8,128)S(1)}, f32[2,128,128]{2,1,0:T(8,128)}, u32[]{:S(2)}) copy-start(f32[2,128,128]{2,1,0:T(8,128)} %param.17) | copy-start | bytes 393220
  25.3 30.5 %all-to-all-start.1 = ((bf16[16,2,128,128]{3,2,1,0:T(8,128)(2,1)}), bf16[16,2,128,128]{3,2,1,0:T(8,128)(2,1)S(1)}, u32[]{:S(2)}, u32[]{:S(2)}) async-start(bf16[16,2,128,128]{3,2,1,0:T(8,128)(2,1)} %scatter_fusion), calls=%async_computation.1 | async-start | bytes 2097152 | tf_op jit(solution)/shard_map/all_to_all | solution.py:153
  30.3 205.7 %all-gather.2.cloned.1.call-start = ((), (), s32[]{:S(2)}) async-start(), calls=%async_computation.2 | async-start | bytes 1179648 | tf_op jit(solution)/shard_map/all_gather | solution.py:159
  118.6 2.4 collective-permute-start
  121.0 3.3 %collective-permute-start.1 = (f32[3,64,256]{2,1,0:T(8,128)S(1)}, f32[3,64,256]{2,1,0:T(8,128)S(1)}, u32[]{:S(2)}, u32[]{:S(2)}) collective-permute-start(f32[3,64,256]{2,1,0:T(8,128)S(1)} %get-tuple-element.153), channel_id=1, source_target_pairs={{8,0},{16,8},{24,16},{9,1},{17,9},{25,17},{10,2},{18,10},{26,18},{... | collective-permute-start | bytes 589832 | tf_op jit(solution)/shard_map/ppermute | solution.py:15
  124.5 4.5 %collective-permute-start.2 = (f32[3,128,64]{2,1,0:T(8,128)S(1)}, f32[3,128,64]{2,1,0:T(8,128)S(1)}, u32[]{:S(2)}, u32[]{:S(2)}) collective-permute-start(f32[3,128,64]{2,1,0:T(8,128)S(1)} %get-tuple-element.152), channel_id=1, source_target_pairs={{0,1},{1,2},{2,3},{3,4},{4,5},{5,6},{6,7},{8,9},{9,10},{10,11},{11... | collective-permute-start | bytes 294920 | tf_op jit(solution)/shard_map/ppermute | solution.py:15
  125.9 59.2 %collective-permute-start.3 = (f32[3,128,64]{2,1,0:T(8,128)S(1)}, f32[3,128,64]{2,1,0:T(8,128)S(1)}, u32[]{:S(2)}, u32[]{:S(2)}) collective-permute-start(f32[3,128,64]{2,1,0:T(8,128)S(1)} %get-tuple-element.151), channel_id=1, source_target_pairs={{1,0},{2,1},{3,2},{4,3},{5,4},{6,5},{7,6},{9,8},{10,9},{11,10},{12... | collective-permute-start | bytes 294920 | tf_op jit(solution)/shard_map/ppermute | solution.py:15
  186.4 6.1 %collective-permute-start.4 = (bf16[2,64,128]{2,1,0:T(8,128)(2,1)S(1)}, bf16[2,64,128]{2,1,0:T(8,128)(2,1)S(1)}, u32[]{:S(2)}, u32[]{:S(2)}) collective-permute-start(bf16[2,64,128]{2,1,0:T(8,128)(2,1)S(1)} %get-tuple-element.161), channel_id=1, source_target_pairs={{0,8},{8,16},{16,24},{1,9},{9,17},{17,25},{2,10},{10,18},{18,26},{... | collective-permute-start | bytes 98312 | tf_op jit(solution)/shard_map/ppermute | solution.py:26
  191.2 3.6 %collective-permute-start.5 = (bf16[2,64,128]{2,1,0:T(8,128)(2,1)S(1)}, bf16[2,64,128]{2,1,0:T(8,128)(2,1)S(1)}, u32[]{:S(2)}, u32[]{:S(2)}) collective-permute-start(bf16[2,64,128]{2,1,0:T(8,128)(2,1)S(1)} %get-tuple-element.162), channel_id=1, source_target_pairs={{8,0},{16,8},{24,16},{9,1},{17,9},{25,17},{10,2},{18,10},{26,18},{... | collective-permute-start | bytes 98312 | tf_op jit(solution)/shard_map/ppermute | solution.py:28
  249.7 2.2 copy-start
Sparse Core Ops, SparseCore 0:
  195.6 40.3 all-gather.1
where the time goes:
time: 267 us; the launch traced here: 266 us
  waiting for transfers between devices  127 us (48%)
  local copies, waits for them, and re-layouts  43.4 us (16%)
  loops' own time  37.5 us (14%)
  starting transfers between devices  23.6 us (9%)
  between operations  14.4 us (5%)
  matrix products  12 us (4%)
  other arithmetic  8.18 us (3%)
    ppermute x4, waiting for transfers between devices, passed_along(): lax.ppermute(value, axis, [(source, source + steps) for source in range(f...  59.5 us
    all_gather x1, waiting for transfers between devices, body(): band_rows = lax.all_gather(strip, 'pos', axis=2, tiled=True)  40.4 us
    another operation x1, loops' own time, accumulate(): lax.fori_loop(0, live_count, add_one, jnp.zeros((3, TS + F, TS + F), jnp....  37.2 us
    all_to_all x1, waiting for transfers between devices, body(): lax.all_to_all(send_wave, 'pos', split_axis=0, concat_axis=0, tiled=True)  23.4 us
    dynamic_update_slice x6, local copies, waits for them, and re-layouts, add_one(): return lax.dynamic_update_slice(canvas, old + piece, where)  17.2 us
    gather x12, local copies, waits for them, and re-layouts  7.71 us
    all_to_all x1, starting transfers between devices, body(): lax.all_to_all(send_meta, 'pos', split_axis=0, concat_axis=0, tiled=True)  7.28 us
  transfers between devices with their start and end apart: 9, of which 8 were waited for; matrix products, arithmetic and copies ran while one was open for 3% of the time, Pallas kernels for 0%

commit v1 on v0

--- a/solution.py
+++ b/solution.py
@@ -7,6 +7,16 @@
 F = 128
 TS = 128
 C = 2
+
+
+def pass_along(array, axis, d):
+    size = lax.axis_size(axis)
+    moving, tiles = (array, [array])
+    for _ in range(size - 1):
+        moving = lax.ppermute(moving, axis, [(i, (i + 1) % size) for i in range(size)])
+        tiles.insert(0, moving)
+    flat = jnp.concatenate(tiles, axis=d)
+    return jnp.roll(flat, (lax.axis_index(axis) + 1) * array.shape[d], axis=d)
 
 
 def passed_along(value, axis, steps):
@@ -156,7 +166,7 @@
     object_tile, ordering, live_count = accumulate(got_wave, got_meta, power_map)
     object_half = object_tile.astype(jnp.bfloat16)
     strip = extended(object_half, (("area", 1),), margin)
-    band_rows = lax.all_gather(strip, "pos", axis=2, tiled=True)
+    band_rows = pass_along(strip, "pos", 2)
     band_rows = jnp.pad(band_rows, ((0, 0), (0, 0), (margin, margin)))
     own_patch = cut_patches(band_rows, offsets[:, 0], target * TS + offsets[:, 1])
     new_wave = relaxed_update(exit_wave, amplitude, own_patch, probe_re, probe_im)

time: 267 us -> 270 us (1.011)
  between operations: 14.4 us -> 1.13 us
  waiting for transfers between devices: 127 us -> 139 us
  starting transfers between devices: 23.6 us -> 26.7 us
    ppermute x0 -> x7, waiting for transfers between devices: none -> 52.1 us  [pass_along(): lax.ppermute(moving, axis, [(i, (i + 1) % size) for i in range(size)])]
    all_gather x1 -> x0, waiting for transfers between devices: 40.4 us -> none  [body(): band_rows = lax.all_gather(strip, 'pos', axis=2, tiled=True)]
    ppermute x0 -> x7, starting transfers between devices: none -> 3.19 us  [pass_along(): lax.ppermute(moving, axis, [(i, (i + 1) % size) for i in range(size)])]
  transfers between devices with their start and end apart: 9 -> 15, of which waited for: 8 -> 14; matrix products, arithmetic and copies ran while one was open for 3% -> 3% of each run, Pallas kernels for 0% -> 0%
where the time goes in v1:
time: 270 us; the launch traced here: 269 us
  waiting for transfers between devices  139 us (51%)
  local copies, waits for them, and re-layouts  43.8 us (16%)
  loops' own time  38.4 us (14%)
  starting transfers between devices  26.7 us (10%)
  matrix products  12 us (4%)
  other arithmetic  7.65 us (3%)
    ppermute x4, waiting for transfers between devices, passed_along(): lax.ppermute(value, axis, [(source, source + steps) for source in range(f...  60.6 us
    ppermute x7, waiting for transfers between devices, pass_along(): lax.ppermute(moving, axis, [(i, (i + 1) % size) for i in range(size)])  52.1 us
    another operation x1, loops' own time, accumulate(): lax.fori_loop(0, live_count, add_one, jnp.zeros((3, TS + F, TS + F), jnp....  38.1 us
    all_to_all x1, waiting for transfers between devices, body(): lax.all_to_all(send_wave, 'pos', split_axis=0, concat_axis=0, tiled=True)  23.4 us
    dynamic_update_slice x6, local copies, waits for them, and re-layouts, add_one(): return lax.dynamic_update_slice(canvas, old + piece, where)  17.2 us
    gather x12, local copies, waits for them, and re-layouts  8.16 us
    all_to_all x1, starting transfers between devices, body(): lax.all_to_all(send_meta, 'pos', split_axis=0, concat_axis=0, tiled=True)  7.28 us
  transfers between devices with their start and end apart: 15, of which 14 were waited for; matrix products, arithmetic and copies ran while one was open for 3% of the time, Pallas kernels for 0%

profile of v1, /device:TPU:0, one launch (start us, length us, event | category | flops | bytes accessed | tf_op | source)
XLA Modules:
  0.0 268.9 jit_solution(9863055999972811696)
XLA Ops:
  1.4 0.8 select_reduce_fusion
  3.8 1.2 scatter_custom_fusion
  4.9 7.3 %all-to-all-start = ((s32[8,2,3]{2,1,0:T(2,128)}), s32[8,2,3]{2,1,0:T(2,128)S(1)}, u32[]{:S(2)}, u32[]{:S(2)}) async-start(s32[8,2,3]{2,1,0:T(2,128)} %bitcast.10), calls=%async_computation | async-start | bytes 16384 | tf_op jit(solution)/shard_map/all_to_all | solution.py:164
  12.2 1.0 copy_convert_fusion
  13.2 0.9 slice_bitcast_fusion.3
  14.2 1.2 broadcast_in_dim.11
  15.4 2.2 scatter_fusion
  17.7 1.1 all-to-all-done
  18.7 4.9 %all-to-all-start.1 = ((bf16[16,2,128,128]{3,2,1,0:T(8,128)(2,1)}), bf16[16,2,128,128]{3,2,1,0:T(8,128)(2,1)S(1)}, u32[]{:S(2)}, u32[]{:S(2)}) async-start(bf16[16,2,128,128]{3,2,1,0:T(8,128)(2,1)} %scatter_fusion), calls=%async_computation.1 | async-start | bytes 2097152 | tf_op jit(solution)/shard_map/all_to_all | solution.py:163
  24.4 1.3 sort.17
  25.7 23.4 %all-to-all-done.1 = bf16[16,2,128,128]{3,2,1,0:T(8,128)(2,1)S(1)} async-done(((bf16[16,2,128,128]{3,2,1,0:T(8,128)(2,1)}), bf16[16,2,128,128]{3,2,1,0:T(8,128)(2,1)S(1)}, u32[]{:S(2)}, u32[]{:S(2)}) %all-to-all-start.1) | async-done | bytes 1048608 | tf_op jit(solution)/shard_map/all_to_all | solution.py:163
  49.2 64.0 %while.15 = (s32[]{:T(128)}, f32[3,256,256]{2,1,0:T(8,128)S(1)}, s32[]{:T(128)}, s32[16]{0:T(128)S(1)}, s32[16,3]{0,1:T(4,128)S(1)}, /*index=5*/bf16[16,2,128,12...) while((s32[]{:T(128)}, f32[3,256,256]{2,1,0:T(8,128)S(1)}, ...), condition=%wide.region_7.8_spmd, body=%wide.region_6.7_spmd.sunk | while | flops 131086 | bytes 1179941 | solution.py:114
  56.8 2.8 %dynamic_update_slice.4 = f32[3,256,256]{2,1,0:T(8,128)S(1)} dynamic-update-slice(f32[3,256,256]{2,1,0:T(8,128)S(1)} %get-tuple-element.257, f32[3,128,128]{2,1,0:T(8,128)S(1)} %maximum_add_fusion.2, s32[]{:T(128)} %constant.176.clone.1..sunk, s32[]{:T(128)S(6)} %select_n.152, s32[]{:T(128)S(6)} %select_n.153) | dynamic-update-slice | bytes 393220 | tf_op jit(solution)/shard_map/while/body/dynamic_update_slice | solution.py:112
  67.3 2.9 %dynamic_update_slice.4 = f32[3,256,256]{2,1,0:T(8,128)S(1)} dynamic-update-slice(f32[3,256,256]{2,1,0:T(8,128)S(1)} %get-tuple-element.257, f32[3,128,128]{2,1,0:T(8,128)S(1)} %maximum_add_fusion.2, s32[]{:T(128)} %constant.176.clone.1..sunk, s32[]{:T(128)S(6)} %select_n.152, s32[]{:T(128)S(6)} %select_n.153) | dynamic-update-slice | bytes 393220 | tf_op jit(solution)/shard_map/while/body/dynamic_update_slice | solution.py:112
  77.9 2.9 %dynamic_update_slice.4 = f32[3,256,256]{2,1,0:T(8,128)S(1)} dynamic-update-slice(f32[3,256,256]{2,1,0:T(8,128)S(1)} %get-tuple-element.257, f32[3,128,128]{2,1,0:T(8,128)S(1)} %maximum_add_fusion.2, s32[]{:T(128)} %constant.176.clone.1..sunk, s32[]{:T(128)S(6)} %select_n.152, s32[]{:T(128)S(6)} %select_n.153) | dynamic-update-slice | bytes 393220 | tf_op jit(solution)/shard_map/while/body/dynamic_update_slice | solution.py:112
  88.5 2.8 %dynamic_update_slice.4 = f32[3,256,256]{2,1,0:T(8,128)S(1)} dynamic-update-slice(f32[3,256,256]{2,1,0:T(8,128)S(1)} %get-tuple-element.257, f32[3,128,128]{2,1,0:T(8,128)S(1)} %maximum_add_fusion.2, s32[]{:T(128)} %constant.176.clone.1..sunk, s32[]{:T(128)S(6)} %select_n.152, s32[]{:T(128)S(6)} %select_n.153) | dynamic-update-slice | bytes 393220 | tf_op jit(solution)/shard_map/while/body/dynamic_update_slice | solution.py:112
  99.0 3.0 %dynamic_update_slice.4 = f32[3,256,256]{2,1,0:T(8,128)S(1)} dynamic-update-slice(f32[3,256,256]{2,1,0:T(8,128)S(1)} %get-tuple-element.257, f32[3,128,128]{2,1,0:T(8,128)S(1)} %maximum_add_fusion.2, s32[]{:T(128)} %constant.176.clone.1..sunk, s32[]{:T(128)S(6)} %select_n.152, s32[]{:T(128)S(6)} %select_n.153) | dynamic-update-slice | bytes 393220 | tf_op jit(solution)/shard_map/while/body/dynamic_update_slice | solution.py:112
  109.7 2.9 %dynamic_update_slice.4 = f32[3,256,256]{2,1,0:T(8,128)S(1)} dynamic-update-slice(f32[3,256,256]{2,1,0:T(8,128)S(1)} %get-tuple-element.257, f32[3,128,128]{2,1,0:T(8,128)S(1)} %maximum_add_fusion.2, s32[]{:T(128)} %constant.176.clone.1..sunk, s32[]{:T(128)S(6)} %select_n.152, s32[]{:T(128)S(6)} %select_n.153) | dynamic-update-slice | bytes 393220 | tf_op jit(solution)/shard_map/while/body/dynamic_update_slice | solution.py:112
  113.2 1.3 collective-permute-start
  114.5 1.0 collective-permute-done
  115.6 1.3 collective-permute-start.1
  116.9 2.0 collective-permute-done.1
  119.1 1.3 collective-permute-start.2
  120.5 1.3 collective-permute-start.3
  121.8 1.8 collective-permute-done.2
  123.7 1.3 scatter-add.16
  125.0 55.7 %collective-permute-done.3 = f32[3,128,64]{2,1,0:T(8,128)S(1)} collective-permute-done((f32[3,128,64]{2,1,0:T(8,128)S(1)}, f32[3,128,64]{2,1,0:T(8,128)S(1)}, u32[]{:S(2)}, u32[]{:S(2)}) %collective-permute-start.3) | collective-permute-done | bytes 98336 | tf_op jit(solution)/shard_map/ppermute | solution.py:25
  182.1 4.8 %collective-permute-start.4 = (bf16[2,64,128]{2,1,0:T(8,128)(2,1)S(1)}, bf16[2,64,128]{2,1,0:T(8,128)(2,1)S(1)}, u32[]{:S(2)}, u32[]{:S(2)}) collective-permute-start(bf16[2,64,128]{2,1,0:T(8,128)(2,1)S(1)} %get-tuple-element.161), channel_id=1, source_target_pairs={{0,8},{8,16},{16,24},{1,9},{9,17},{17,25},{2,10},{10,18},{18,26},{... | collective-permute-start | bytes 98312 | tf_op jit(solution)/shard_map/ppermute | solution.py:36
  186.8 1.3 collective-permute-start.5
  188.2 2.3 collective-permute-done.5
  190.5 3.0 %collective-permute-start.6 = (bf16[2,256,128]{2,1,0:T(8,128)(2,1)S(1)}, bf16[2,256,128]{2,1,0:T(8,128)(2,1)S(1)}, u32[]{:S(2)}, u32[]{:S(2)}) collective-permute-start(bf16[2,256,128]{2,1,0:T(8,128)(2,1)S(1)} %pad_maximum_fusion.2), channel_id=1, source_target_pairs={{0,1},{1,2},{2,3},{3,4},{4,5},{5,6},{6,7},{7,0},{8,9},{9,10},{10,1... | collective-permute-start | bytes 393224 | tf_op jit(solution)/shard_map/ppermute | solution.py:16
  193.4 4.8 %collective-permute-done.6 = bf16[2,256,128]{2,1,0:T(8,128)(2,1)S(1)} collective-permute-done((bf16[2,256,128]{2,1,0:T(8,128)(2,1)S(1)}, bf16[2,256,128]{2,1,0:T(8,128)(2,1)S(1)}, u32[]{:S(2)}, u32[]{:S(2)}) %collective-permute-start.6) | collective-permute-done | bytes 131104 | tf_op jit(solution)/shard_map/ppermute | solution.py:16
  198.4 8.3 %collective-permute-done.7 = bf16[2,256,128]{2,1,0:T(8,128)(2,1)S(1)} collective-permute-done((bf16[2,256,128]{2,1,0:T(8,128)(2,1)S(1)}, bf16[2,256,128]{2,1,0:T(8,128)(2,1)S(1)}, u32[]{:S(2)}, u32[]{:S(2)}) %collective-permute-start.7) | collective-permute-done | bytes 131104 | tf_op jit(solution)/shard_map/ppermute | solution.py:16
  206.7 8.4 %collective-permute-done.8 = bf16[2,256,128]{2,1,0:T(8,128)(2,1)S(1)} collective-permute-done((bf16[2,256,128]{2,1,0:T(8,128)(2,1)S(1)}, bf16[2,256,128]{2,1,0:T(8,128)(2,1)S(1)}, u32[]{:S(2)}, u32[]{:S(2)}) %collective-permute-start.8) | collective-permute-done | bytes 131104 | tf_op jit(solution)/shard_map/ppermute | solution.py:16
  215.2 7.7 %collective-permute-done.9 = bf16[2,256,128]{2,1,0:T(8,128)(2,1)S(1)} collective-permute-done((bf16[2,256,128]{2,1,0:T(8,128)(2,1)S(1)}, bf16[2,256,128]{2,1,0:T(8,128)(2,1)S(1)}, u32[]{:S(2)}, u32[]{:S(2)}) %collective-permute-start.9) | collective-permute-done | bytes 131104 | tf_op jit(solution)/shard_map/ppermute | solution.py:16
  222.8 7.7 %collective-permute-done.10 = bf16[2,256,128]{2,1,0:T(8,128)(2,1)S(1)} collective-permute-done((bf16[2,256,128]{2,1,0:T(8,128)(2,1)S(1)}, bf16[2,256,128]{2,1,0:T(8,128)(2,1)S(1)}, u32[]{:S(2)}, u32[]{:S(2)}) %collective-permute-start.10) | collective-permute-done | bytes 131104 | tf_op jit(solution)/shard_map/ppermute | solution.py:16
  230.5 7.7 %collective-permute-done.11 = bf16[2,256,128]{2,1,0:T(8,128)(2,1)S(1)} collective-permute-done((bf16[2,256,128]{2,1,0:T(8,128)(2,1)S(1)}, bf16[2,256,128]{2,1,0:T(8,128)(2,1)S(1)}, u32[]{:S(2)}, u32[]{:S(2)}) %collective-permute-start.11) | collective-permute-done | bytes 131104 | tf_op jit(solution)/shard_map/ppermute | solution.py:16
  238.3 7.5 %collective-permute-done.12 = bf16[2,256,128]{2,1,0:T(8,128)(2,1)S(1)} collective-permute-done((bf16[2,256,128]{2,1,0:T(8,128)(2,1)S(1)}, bf16[2,256,128]{2,1,0:T(8,128)(2,1)S(1)}, u32[]{:S(2)}, u32[]{:S(2)}) %collective-permute-start.12) | collective-permute-done | bytes 131104 | tf_op jit(solution)/shard_map/ppermute | solution.py:16
  246.7 0.8 pad.13
  247.5 8.4 %while.16 = (s32[]{:T(128)}, bf16[2,256,1152]{2,1,0:T(8,128)(2,1)S(1)}, s32[4,3]{1,0:T(4,128)S(1)}, bf16[4,2,128,128]{3,2,0,1:T(8,128)(2,1)S(1)}, s32[]{:T(128)}) while((s32[]{:T(128)}, bf16[2,256,1152]{2,1,0:T(8,128)(2,1)S(1)}, s32[4,3]{1,0:T(4,128)S(1)}, bf16[4,2,128,128]{3,2,0,1:T(8,128)(2,1)S(1)}, s32[]{:T(128)}) %tuple.76), condition=%wide.while_cond.4, body=%wide.while_body.4.sunk | while | flops 2 | bytes 131189 | solution.py:90
  248.1 1.4 bitcast_dynamic-update-slice_fusion.2
  250.2 1.4 bitcast_dynamic-update-slice_fusion.2
  252.3 1.4 bitcast_dynamic-update-slice_fusion.2
  254.3 1.4 bitcast_dynamic-update-slice_fusion.2
  262.0 0.8 fusion.34
  262.8 0.8 fusion.38
  263.6 0.8 fusion.5
  265.8 0.8 fusion.4
  (104 shorter events, 27.0 us)
Async XLA Ops:
  4.9 13.8 %all-to-all-start = ((s32[8,2,3]{2,1,0:T(2,128)}), s32[8,2,3]{2,1,0:T(2,128)S(1)}, u32[]{:S(2)}, u32[]{:S(2)}) async-start(s32[8,2,3]{2,1,0:T(2,128)} %bitcast.10), calls=%async_computation | async-start | bytes 16384 | tf_op jit(solution)/shard_map/all_to_all | solution.py:164
  14.2 9.4 %copy-start.1 = (f32[2,128,128]{2,1,0:T(8,128)S(1)}, f32[2,128,128]{2,1,0:T(8,128)}, u32[]{:S(2)}) copy-start(f32[2,128,128]{2,1,0:T(8,128)} %param.17) | copy-start | bytes 393220
  18.7 30.4 %all-to-all-start.1 = ((bf16[16,2,128,128]{3,2,1,0:T(8,128)(2,1)}), bf16[16,2,128,128]{3,2,1,0:T(8,128)(2,1)S(1)}, u32[]{:S(2)}, u32[]{:S(2)}) async-start(bf16[16,2,128,128]{3,2,1,0:T(8,128)(2,1)} %scatter_fusion), calls=%async_computation.1 | async-start | bytes 2097152 | tf_op jit(solution)/shard_map/all_to_all | solution.py:163
  113.2 2.4 collective-permute-start
  115.6 3.3 %collective-permute-start.1 = (f32[3,64,256]{2,1,0:T(8,128)S(1)}, f32[3,64,256]{2,1,0:T(8,128)S(1)}, u32[]{:S(2)}, u32[]{:S(2)}) collective-permute-start(f32[3,64,256]{2,1,0:T(8,128)S(1)} %get-tuple-element.153), channel_id=1, source_target_pairs={{8,0},{16,8},{24,16},{9,1},{17,9},{25,17},{10,2},{18,10},{26,18},{... | collective-permute-start | bytes 589832 | tf_op jit(solution)/shard_map/ppermute | solution.py:25
  119.1 4.5 %collective-permute-start.2 = (f32[3,128,64]{2,1,0:T(8,128)S(1)}, f32[3,128,64]{2,1,0:T(8,128)S(1)}, u32[]{:S(2)}, u32[]{:S(2)}) collective-permute-start(f32[3,128,64]{2,1,0:T(8,128)S(1)} %get-tuple-element.152), channel_id=1, source_target_pairs={{0,1},{1,2},{2,3},{3,4},{4,5},{5,6},{6,7},{8,9},{9,10},{10,11},{11... | collective-permute-start | bytes 294920 | tf_op jit(solution)/shard_map/ppermute | solution.py:25
  120.5 60.2 %collective-permute-start.3 = (f32[3,128,64]{2,1,0:T(8,128)S(1)}, f32[3,128,64]{2,1,0:T(8,128)S(1)}, u32[]{:S(2)}, u32[]{:S(2)}) collective-permute-start(f32[3,128,64]{2,1,0:T(8,128)S(1)} %get-tuple-element.151), channel_id=1, source_target_pairs={{1,0},{2,1},{3,2},{4,3},{5,4},{6,5},{7,6},{9,8},{10,9},{11,10},{12... | collective-permute-start | bytes 294920 | tf_op jit(solution)/shard_map/ppermute | solution.py:25
  182.1 6.1 %collective-permute-start.4 = (bf16[2,64,128]{2,1,0:T(8,128)(2,1)S(1)}, bf16[2,64,128]{2,1,0:T(8,128)(2,1)S(1)}, u32[]{:S(2)}, u32[]{:S(2)}) collective-permute-start(bf16[2,64,128]{2,1,0:T(8,128)(2,1)S(1)} %get-tuple-element.161), channel_id=1, source_target_pairs={{0,8},{8,16},{16,24},{1,9},{9,17},{17,25},{2,10},{10,18},{18,26},{... | collective-permute-start | bytes 98312 | tf_op jit(solution)/shard_map/ppermute | solution.py:36
  186.8 3.6 %collective-permute-start.5 = (bf16[2,64,128]{2,1,0:T(8,128)(2,1)S(1)}, bf16[2,64,128]{2,1,0:T(8,128)(2,1)S(1)}, u32[]{:S(2)}, u32[]{:S(2)}) collective-permute-start(bf16[2,64,128]{2,1,0:T(8,128)(2,1)S(1)} %get-tuple-element.162), channel_id=1, source_target_pairs={{8,0},{16,8},{24,16},{9,1},{17,9},{25,17},{10,2},{18,10},{26,18},{... | collective-permute-start | bytes 98312 | tf_op jit(solution)/shard_map/ppermute | solution.py:38
  190.5 7.7 %collective-permute-start.6 = (bf16[2,256,128]{2,1,0:T(8,128)(2,1)S(1)}, bf16[2,256,128]{2,1,0:T(8,128)(2,1)S(1)}, u32[]{:S(2)}, u32[]{:S(2)}) collective-permute-start(bf16[2,256,128]{2,1,0:T(8,128)(2,1)S(1)} %pad_maximum_fusion.2), channel_id=1, source_target_pairs={{0,1},{1,2},{2,3},{3,4},{4,5},{5,6},{6,7},{7,0},{8,9},{9,10},{10,1... | collective-permute-start | bytes 393224 | tf_op jit(solution)/shard_map/ppermute | solution.py:16
  198.2 8.6 %collective-permute-start.7 = (bf16[2,256,128]{2,1,0:T(8,128)(2,1)S(1)}, bf16[2,256,128]{2,1,0:T(8,128)(2,1)S(1)}, u32[]{:S(2)}, u32[]{:S(2)}) collective-permute-start(bf16[2,256,128]{2,1,0:T(8,128)(2,1)S(1)} %collective-permute-done.6), channel_id=1, source_target_pairs={{0,1},{1,2},{2,3},{3,4},{4,5},{5,6},{6,7},{7,0},{8,9},{9,10},{10,1... | collective-permute-start | bytes 393224 | tf_op jit(solution)/shard_map/ppermute | solution.py:16
  206.7 8.4 %collective-permute-start.8 = (bf16[2,256,128]{2,1,0:T(8,128)(2,1)S(1)}, bf16[2,256,128]{2,1,0:T(8,128)(2,1)S(1)}, u32[]{:S(2)}, u32[]{:S(2)}) collective-permute-start(bf16[2,256,128]{2,1,0:T(8,128)(2,1)S(1)} %collective-permute-done.7), channel_id=1, source_target_pairs={{0,1},{1,2},{2,3},{3,4},{4,5},{5,6},{6,7},{7,0},{8,9},{9,10},{10,1... | collective-permute-start | bytes 393224 | tf_op jit(solution)/shard_map/ppermute | solution.py:16
  215.2 7.7 %collective-permute-start.9 = (bf16[2,256,128]{2,1,0:T(8,128)(2,1)S(1)}, bf16[2,256,128]{2,1,0:T(8,128)(2,1)S(1)}, u32[]{:S(2)}, u32[]{:S(2)}) collective-permute-start(bf16[2,256,128]{2,1,0:T(8,128)(2,1)S(1)} %collective-permute-done.8), channel_id=1, source_target_pairs={{0,1},{1,2},{2,3},{3,4},{4,5},{5,6},{6,7},{7,0},{8,9},{9,10},{10,1... | collective-permute-start | bytes 393224 | tf_op jit(solution)/shard_map/ppermute | solution.py:16
  222.8 7.7 %collective-permute-start.10 = (bf16[2,256,128]{2,1,0:T(8,128)(2,1)S(1)}, bf16[2,256,128]{2,1,0:T(8,128)(2,1)S(1)}, u32[]{:S(2)}, u32[]{:S(2)}) collective-permute-start(bf16[2,256,128]{2,1,0:T(8,128)(2,1)S(1)} %collective-permute-done.9), channel_id=1, source_target_pairs={{0,1},{1,2},{2,3},{3,4},{4,5},{5,6},{6,7},{7,0},{8,9},{9,10},{10,1... | collective-permute-start | bytes 393224 | tf_op jit(solution)/shard_map/ppermute | solution.py:16
  230.5 7.7 %collective-permute-start.11 = (bf16[2,256,128]{2,1,0:T(8,128)(2,1)S(1)}, bf16[2,256,128]{2,1,0:T(8,128)(2,1)S(1)}, u32[]{:S(2)}, u32[]{:S(2)}) collective-permute-start(bf16[2,256,128]{2,1,0:T(8,128)(2,1)S(1)} %collective-permute-done.10), channel_id=1, source_target_pairs={{0,1},{1,2},{2,3},{3,4},{4,5},{5,6},{6,7},{7,0},{8,9},{9,10},{10,1... | collective-permute-start | bytes 393224 | tf_op jit(solution)/shard_map/ppermute | solution.py:16
  238.2 7.7 %collective-permute-start.12 = (bf16[2,256,128]{2,1,0:T(8,128)(2,1)S(1)}, bf16[2,256,128]{2,1,0:T(8,128)(2,1)S(1)}, u32[]{:S(2)}, u32[]{:S(2)}) collective-permute-start(bf16[2,256,128]{2,1,0:T(8,128)(2,1)S(1)} %collective-permute-done.11), channel_id=1, source_target_pairs={{0,1},{1,2},{2,3},{3,4},{4,5},{5,6},{6,7},{7,0},{8,9},{9,10},{10,1... | collective-permute-start | bytes 393224 | tf_op jit(solution)/shard_map/ppermute | solution.py:16
  258.3 3.7 %copy-start = (bf16[4,128,128]{2,1,0:T(8,128)(2,1)S(1)}, bf16[4,128,128]{2,1,0:T(8,128)(2,1)}, u32[]{:S(2)}) copy-start(bf16[4,128,128]{2,1,0:T(8,128)(2,1)} %param.16) | copy-start | bytes 393220
